TPU v7x, 32 devices: a whole 2x2x4 slice. The times are simulated.
32 devices in a mesh: dp: 8 (over y, x, core), mp: 4 (over z).
Axes of the slice: x: 2, y: 2, z: 4, core: 2. Of those that a mesh axis runs over, the one named last changes fastest.
Arguments:
- hidden: bfloat16 [4096, 768], P('dp'), may hold values from -6 to 6
- memory: bfloat16 [32768, 768], P('dp', 'mp'), may hold values from -6 to 6
- out_grad: bfloat16 [4096, 768], P('dp'), may hold values from -6 to 6
- dec_starts: int32 [32, 4], P('dp'), may hold values from 0 to 127, as said below
- dec_length: int32 [32], P('dp'), may hold values from 96 to 128
- mem_starts: int32 [32, 4], P('dp'), may hold values from 0 to 1023, as said below
- mem_length: int32 [32], P('dp'), may hold values from 768 to 1024
- self_qkv: bfloat16 [3, 768, 768], P(None, None, 'mp'), may hold values from -0.25 to 0.25
- self_qv_bias: float32 [2, 768], P(None, 'mp'), may hold values from -3 to 3
- self_proj: bfloat16 [768, 768], P('mp'), may hold values from -0.3125 to 0.3125
- cross_query: bfloat16 [768, 768], P(None, 'mp'), may hold values from -0.25 to 0.25
- cross_kv: bfloat16 [2, 768, 768], P(None, None, 'mp'), may hold values from -0.25 to 0.25
- cross_qv_bias: float32 [2, 768], P(None, 'mp'), may hold values from -3 to 3
- cross_proj: bfloat16 [768, 768], P('mp'), may hold values from -0.875 to 0.875
- ffn_in: bfloat16 [768, 3072], P(None, 'mp'), may hold values from -0.21875 to 0.21875
- ffn_in_bias: float32 [3072], P('mp'), may hold values from -3 to 3
- ffn_out: bfloat16 [3072, 768], P('mp'), may hold values from -0.15625 to 0.15625
- out_biases: float32 [3, 768], replicated, may hold values from -3 to 3
- norm_gains: float32 [3, 768], replicated, may hold values from 0.25 to 1.75
- norm_biases: float32 [3, 768], replicated, may hold values from -2 to 2
Outputs:
- result: bfloat16 [4096, 768], P('dp')
- hidden_grad: float32 [4096, 768], P('dp')
- memory_grad: float32 [32768, 768], P('dp', 'mp')
- self_qkv_grad: float32 [3, 768, 768], P(None, None, 'mp')
- self_qv_bias_grad: float32 [2, 768], P(None, 'mp')
- self_proj_grad: float32 [768, 768], P('mp')
- cross_query_grad: float32 [768, 768], P(None, 'mp')
- cross_kv_grad: float32 [2, 768, 768], P(None, None, 'mp')
- cross_qv_bias_grad: float32 [2, 768], P(None, 'mp')
- cross_proj_grad: float32 [768, 768], P('mp')
- ffn_in_grad: float32 [768, 3072], P(None, 'mp')
- ffn_in_bias_grad: float32 [3072], P('mp')
- ffn_out_grad: float32 [3072, 768], P('mp')
- out_biases_grad: float32 [3, 768], replicated
- norm_gains_grad: float32 [3, 768], replicated
- norm_biases_grad: float32 [3, 768], replicated
Inputs may be any that keep to these rules, and one draw needn't show every extreme that they name: `dec_starts`: each packed row holds 4 pairs; its offsets start at 0, rise strictly and stay below the row's used slots, so every decoder segment holds at least one used slot; padded slots belong to the last pair. `mem_starts`: pair j's table is memory segment j of the same packed row; offsets start at 0, rise strictly and stay below the row's used slots, so every memory segment holds at least one used slot.
All inputs are finite; a program needn't handle non-finite values.
Results may differ from a plain program's by a relative error of at most 0.023.
Values may be sent and summed in bfloat16 or wider, within the bound.
No kernel may reach another device: no remote copies, remote signals or barrier semaphores. Data moves between devices by JAX's collectives and lax.ppermute only.
A program may use at most 128 MiB of HBM per device.

v0:
```python
import jax
import jax.numpy as jnp
from jax import lax
from jax.sharding import PartitionSpec as P

HD = 64
NEG_FILL = -1000000000.0
EPSILON = 1e-05


def layer_norm(values, gain_row, bias_row):
    average = jnp.mean(values, -1, keepdims=True)
    centered = values - average
    variance = jnp.mean(centered * centered, -1, keepdims=True)
    return centered * lax.rsqrt(variance + EPSILON) * gain_row + bias_row


def exact_gelu(values):
    return jax.nn.gelu(values, approximate=False)


def segment_ids(starts, slot_count):
    places = jnp.arange(slot_count, dtype=jnp.int32)
    return jnp.sum((starts[:, None, :] <= places[None, :, None]).astype(jnp.int32), -1) - 1


def inner_dot(left_side, right_side):
    return lax.dot_general(
        left_side, right_side, (((0,), (0,)), ((), ())), preferred_element_type=jnp.float32
    )


def outer_dot(left_side, right_side):
    return lax.dot_general(
        left_side, right_side, (((1,), (1,)), ((), ())), preferred_element_type=jnp.float32
    )


def row_groups(kernel, arrays):
    row_count = arrays[0].shape[0]
    limit = max(1, 512 // arrays[0].shape[1])
    group_rows = max(
        (count for count in range(1, min(row_count, limit) + 1) if row_count % count == 0)
    )
    blocks = row_count // group_rows
    shaped = tuple((member.reshape((blocks, group_rows) + member.shape[1:]) for member in arrays))
    results = lax.map(lambda pieces: kernel(*pieces), shaped)
    return jax.tree.map(lambda member: member.reshape((row_count,) + member.shape[2:]), results)


def attend_block(queries, key_rows, value_rows, allowed):
    scores = jnp.einsum("rqhd,rkhd->rhqk", queries, key_rows, preferred_element_type=jnp.float32)
    scores = jnp.where(allowed[:, None], scores, NEG_FILL)
    peak_score = jnp.max(scores, -1, keepdims=True)
    weights = jnp.exp(scores - peak_score)
    totals = jnp.sum(weights, -1, keepdims=True)
    prob_low = (weights / totals).astype(jnp.bfloat16)
    output = jnp.einsum("rhqk,rkhd->rqhd", prob_low, value_rows, preferred_element_type=jnp.float32)
    return (output, (peak_score + jnp.log(totals))[..., 0])


def attend_back(queries, key_rows, value_rows, allowed, log_total, grad_rows):
    scores = jnp.einsum("rqhd,rkhd->rhqk", queries, key_rows, preferred_element_type=jnp.float32)
    scores = jnp.where(allowed[:, None], scores, NEG_FILL)
    prob_full = jnp.exp(scores - log_total[..., None])
    prob_low = prob_full.astype(jnp.bfloat16)
    value_grad = jnp.einsum(
        "rhqk,rqhd->rkhd", prob_low, grad_rows, preferred_element_type=jnp.float32
    )
    prob_grad = jnp.einsum(
        "rqhd,rkhd->rhqk", grad_rows, value_rows, preferred_element_type=jnp.float32
    )
    offset = jnp.sum(prob_full * prob_grad, -1, keepdims=True)
    score_grad = (prob_full * (prob_grad - offset)).astype(jnp.bfloat16)
    query_grad = jnp.einsum(
        "rhqk,rkhd->rqhd", score_grad, key_rows, preferred_element_type=jnp.float32
    )
    key_grad = jnp.einsum(
        "rhqk,rqhd->rkhd", score_grad, queries, preferred_element_type=jnp.float32
    )
    return (query_grad, key_grad, value_grad)


def body(
    hidden,
    memory,
    out_grad,
    dec_starts,
    dec_length,
    mem_starts,
    mem_length,
    self_qkv,
    self_qv_bias,
    self_proj,
    cross_query,
    cross_kv,
    cross_qv_bias,
    cross_proj,
    ffn_in,
    ffn_in_bias,
    ffn_out,
    out_biases,
    norm_gains,
    norm_biases,
):
    row_count = dec_starts.shape[0]
    dec_slots = hidden.shape[0] // row_count
    mem_slots = memory.shape[0] // row_count
    local_width = self_qkv.shape[2]
    head_count = local_width // HD
    scaling = HD ** (-0.5)
    dec_places = jnp.arange(dec_slots, dtype=jnp.int32)
    mem_places = jnp.arange(mem_slots, dtype=jnp.int32)
    dec_segment = segment_ids(dec_starts, dec_slots)
    mem_segment = segment_ids(mem_starts, mem_slots)
    self_allowed = (
        (dec_segment[:, :, None] == dec_segment[:, None, :])
        & (dec_places[None, None, :] <= dec_places[None, :, None])
        & (dec_places[None, None, :] < dec_length[:, None, None])
    )
    cross_allowed = (dec_segment[:, :, None] == mem_segment[:, None, :]) & (
        mem_places[None, None, :] < mem_length[:, None, None]
    )

    def split_heads(values):
        return values.reshape(row_count, values.shape[0] // row_count, head_count, HD)

    def merge_heads(values):
        return values.reshape(row_count * values.shape[1], local_width)

    self_weight = jnp.concatenate([self_qkv[0], self_qkv[1], self_qkv[2]], axis=1)
    projected = jnp.dot(hidden, self_weight, preferred_element_type=jnp.float32)
    self_q = split_heads(
        ((projected[:, :local_width] + self_qv_bias[0]) * scaling).astype(jnp.bfloat16)
    )
    self_k = split_heads(projected[:, local_width : 2 * local_width].astype(jnp.bfloat16))
    self_v = split_heads((projected[:, 2 * local_width :] + self_qv_bias[1]).astype(jnp.bfloat16))
    self_out, self_total = row_groups(attend_block, (self_q, self_k, self_v, self_allowed))
    self_low = merge_heads(self_out).astype(jnp.bfloat16)
    self_branch = lax.psum(jnp.dot(self_low, self_proj, preferred_element_type=jnp.float32), "mp")
    first, first_back = jax.vjp(
        layer_norm,
        hidden.astype(jnp.float32) + self_branch + out_biases[0],
        norm_gains[0],
        norm_biases[0],
    )
    first_low = first.astype(jnp.bfloat16)
    cross_pre = jnp.dot(first_low, cross_query, preferred_element_type=jnp.float32)
    cross_q = split_heads(((cross_pre + cross_qv_bias[0]) * scaling).astype(jnp.bfloat16))
    memory_whole = lax.all_gather(memory, "mp", axis=1, tiled=True)
    kv_weight = jnp.concatenate([cross_kv[0], cross_kv[1]], axis=1)
    memory_kv = jnp.dot(memory_whole, kv_weight, preferred_element_type=jnp.float32)
    cross_k = split_heads(memory_kv[:, :local_width].astype(jnp.bfloat16))
    cross_v = split_heads((memory_kv[:, local_width:] + cross_qv_bias[1]).astype(jnp.bfloat16))
    cross_out, cross_total = row_groups(attend_block, (cross_q, cross_k, cross_v, cross_allowed))
    cross_low = merge_heads(cross_out).astype(jnp.bfloat16)
    cross_branch = lax.psum(
        jnp.dot(cross_low, cross_proj, preferred_element_type=jnp.float32), "mp"
    )
    second, second_back = jax.vjp(
        layer_norm, first + cross_branch + out_biases[1], norm_gains[1], norm_biases[1]
    )
    second_low = second.astype(jnp.bfloat16)
    hidden_pre = jnp.dot(second_low, ffn_in, preferred_element_type=jnp.float32) + ffn_in_bias
    activated, gelu_back = jax.vjp(exact_gelu, hidden_pre)
    activated_low = activated.astype(jnp.bfloat16)
    ffn_branch = lax.psum(jnp.dot(activated_low, ffn_out, preferred_element_type=jnp.float32), "mp")
    final_norm, third_back = jax.vjp(
        layer_norm, second + ffn_branch + out_biases[2], norm_gains[2], norm_biases[2]
    )
    third_grad, gain_three, shift_three = third_back(out_grad.astype(jnp.float32))
    third_low = third_grad.astype(jnp.bfloat16)
    ffn_out_grad = inner_dot(activated_low, third_low)
    ffn_bias_out = jnp.sum(third_grad, 0)
    (pre_grad,) = gelu_back(outer_dot(third_low, ffn_out))
    ffn_in_bias_grad = jnp.sum(pre_grad, 0)
    pre_low = pre_grad.astype(jnp.bfloat16)
    ffn_in_grad = inner_dot(second_low, pre_low)
    second_grad = third_grad + lax.psum(outer_dot(pre_low, ffn_in), "mp")
    cross_grad, gain_two, shift_two = second_back(second_grad)
    cross_grad_low = cross_grad.astype(jnp.bfloat16)
    cross_proj_grad = inner_dot(cross_low, cross_grad_low)
    cross_bias_out = jnp.sum(cross_grad, 0)
    cross_out_grad = split_heads(outer_dot(cross_grad_low, cross_proj).astype(jnp.bfloat16))
    cq_grad, ck_grad, cv_grad = row_groups(
        attend_back, (cross_q, cross_k, cross_v, cross_allowed, cross_total, cross_out_grad)
    )
    cq_grad = merge_heads(cq_grad) * scaling
    cv_grad = merge_heads(cv_grad)
    cross_qv_grad = jnp.stack([jnp.sum(cq_grad, 0), jnp.sum(cv_grad, 0)])
    cq_low = cq_grad.astype(jnp.bfloat16)
    cross_query_grad = inner_dot(first_low, cq_low)
    first_grad = cross_grad + lax.psum(outer_dot(cq_low, cross_query), "mp")
    kv_grad_low = jnp.concatenate([merge_heads(ck_grad), cv_grad], axis=1).astype(jnp.bfloat16)
    kv_weight_grad = inner_dot(memory_whole, kv_grad_low)
    cross_kv_grad = jnp.stack([kv_weight_grad[:, :local_width], kv_weight_grad[:, local_width:]])
    memory_grad = lax.psum_scatter(
        outer_dot(kv_grad_low, kv_weight).astype(jnp.bfloat16),
        "mp",
        scatter_dimension=1,
        tiled=True,
    ).astype(jnp.float32)
    self_grad, gain_one, shift_one = first_back(first_grad)
    self_grad_low = self_grad.astype(jnp.bfloat16)
    self_proj_grad = inner_dot(self_low, self_grad_low)
    self_bias_out = jnp.sum(self_grad, 0)
    self_out_grad = split_heads(outer_dot(self_grad_low, self_proj).astype(jnp.bfloat16))
    sq_grad, sk_grad, sv_grad = row_groups(
        attend_back, (self_q, self_k, self_v, self_allowed, self_total, self_out_grad)
    )
    sq_grad = merge_heads(sq_grad) * scaling
    sv_grad = merge_heads(sv_grad)
    self_qv_grad = jnp.stack([jnp.sum(sq_grad, 0), jnp.sum(sv_grad, 0)])
    qkv_low = jnp.concatenate([sq_grad, merge_heads(sk_grad), sv_grad], axis=1).astype(jnp.bfloat16)
    qkv_weight_grad = inner_dot(hidden, qkv_low)
    self_qkv_grad = jnp.stack(
        [
            qkv_weight_grad[:, :local_width],
            qkv_weight_grad[:, local_width : 2 * local_width],
            qkv_weight_grad[:, 2 * local_width :],
        ]
    )
    hidden_grad = self_grad + lax.psum(
        outer_dot(qkv_low, self_weight).astype(jnp.bfloat16), "mp"
    ).astype(jnp.float32)
    (
        self_qkv_grad,
        self_qv_grad,
        self_proj_grad,
        cross_query_grad,
        cross_kv_grad,
        cross_qv_grad,
        cross_proj_grad,
        ffn_in_grad,
        ffn_in_bias_grad,
        ffn_out_grad,
        self_bias_out,
        cross_bias_out,
        ffn_bias_out,
        gain_one,
        gain_two,
        gain_three,
        shift_one,
        shift_two,
        shift_three,
    ) = lax.psum(
        (
            self_qkv_grad,
            self_qv_grad,
            self_proj_grad,
            cross_query_grad,
            cross_kv_grad,
            cross_qv_grad,
            cross_proj_grad,
            ffn_in_grad,
            ffn_in_bias_grad,
            ffn_out_grad,
            self_bias_out,
            cross_bias_out,
            ffn_bias_out,
            gain_one,
            gain_two,
            gain_three,
            shift_one,
            shift_two,
            shift_three,
        ),
        "dp",
    )
    out_biases_grad = jnp.stack([self_bias_out, cross_bias_out, ffn_bias_out])
    norm_gains_grad = jnp.stack([gain_one, gain_two, gain_three])
    norm_biases_grad = jnp.stack([shift_one, shift_two, shift_three])
    return (
        final_norm.astype(jnp.bfloat16),
        hidden_grad,
        memory_grad,
        self_qkv_grad,
        self_qv_grad,
        self_proj_grad,
        cross_query_grad,
        cross_kv_grad,
        cross_qv_grad,
        cross_proj_grad,
        ffn_in_grad,
        ffn_in_bias_grad,
        ffn_out_grad,
        out_biases_grad,
        norm_gains_grad,
        norm_biases_grad,
    )


def solution(mesh):
    placed = (
        P("dp", None),
        P("dp", "mp"),
        P("dp", None),
        P("dp", None),
        P("dp"),
        P("dp", None),
        P("dp"),
        P(None, None, "mp"),
        P(None, "mp"),
        P("mp", None),
        P(None, "mp"),
        P(None, None, "mp"),
        P(None, "mp"),
        P("mp", None),
        P(None, "mp"),
        P("mp"),
        P("mp", None),
        P(),
        P(),
        P(),
    )
    return jax.shard_map(
        body,
        mesh=mesh,
        in_specs=placed,
        out_specs=(
            P("dp", None),
            P("dp", None),
            P("dp", "mp"),
            P(None, None, "mp"),
            P(None, "mp"),
            P("mp", None),
            P(None, "mp"),
            P(None, None, "mp"),
            P(None, "mp"),
            P("mp", None),
            P(None, "mp"),
            P("mp"),
            P("mp", None),
            P(),
            P(),
            P(),
        ),
        check_vma=False,
    )
```

profile of v0, /device:TPU:0, one launch (start us, length us, event | category | flops | bytes accessed | tf_op | source)
XLA Modules:
  0.0 875.1 jit_solution(11104530872102401639)
XLA Ops:
  8.2 1.2 slice_bitcast_fusion.9
  13.4 1.6 fusion.63
  17.6 69.4 %all-reduce.10.cloned.1.call-done = f32[512,768]{1,0:T(8,128)} async-done(((f32[512,768]{1,0:T(8,128)}), f32[512,768]{1,0:T(8,128)}) %all-reduce.10.cloned.1.call-update) | async-done | bytes 1572880 | tf_op jit(solution)/shard_map/psum | solution.py:140
  87.0 1.9 fusion.103
  90.5 1.1 fusion.33
  92.5 110.5 %all-gather.2.cloned.1.call-done = bf16[4096,768]{0,1:T(8,128)(2,1)} async-done(((bf16[4096,192]{0,1:T(8,128)(2,1)}), bf16[4096,768]{0,1:T(8,128)(2,1)}) %all-gather.2.cloned.1.call-update) | async-done | bytes 6291472 | tf_op jit(solution)/shard_map/all_gather | solution.py:150
  203.0 4.8 convolution_bitcast_fusion
  207.8 2.6 copy-done.17
  210.5 1.3 slice.156
  211.8 3.9 squeeze.90
  215.7 3.4 fusion.4
  219.0 3.9 squeeze.88
  222.9 3.5 select_reduce_fusion
  226.4 1.6 fusion
  229.1 2.8 fusion.39
  232.0 1.6 fusion.59
  233.8 67.3 %all-reduce.12.cloned.1.call-done = f32[512,768]{1,0:T(8,128)} async-done(((f32[512,768]{1,0:T(8,128)}), f32[512,768]{1,0:T(8,128)}) %all-reduce.12.cloned.1.call-update) | async-done | bytes 1572880 | tf_op jit(solution)/shard_map/psum | solution.py:157
  301.1 2.0 fusion.102
  303.8 5.4 multiply_convert_fusion.1
  310.1 1.9 fusion.115
  312.1 68.3 %all-reduce.14.cloned.1.call-done = f32[512,768]{1,0:T(8,128)} async-done(((f32[512,768]{1,0:T(8,128)}), f32[512,768]{1,0:T(8,128)}) %all-reduce.14.cloned.1.call-update) | async-done | bytes 1572880 | tf_op jit(solution)/shard_map/psum | solution.py:167
  380.4 2.0 fusion.100
  384.2 1.6 fusion.99
  386.7 1.8 fusion.110
  389.5 2.0 fusion.51
  391.6 68.2 %all-reduce.16.cloned.1.call-done = f32[512,768]{1,0:T(8,128)} async-done(((f32[512,768]{1,0:T(8,128)}), f32[512,768]{1,0:T(8,128)}) %all-reduce.16.cloned.1.call-update) | async-done | bytes 1572880 | tf_op jit(solution)/shard_map/psum | solution.py:179
  459.8 2.8 multiply_reduce_fusion.1
  463.3 1.2 copy-done.10
  465.0 6.5 multiply_reduce_fusion
  471.5 1.8 multiply_convert_fusion
  473.4 2.1 fusion.104
  475.6 1.6 fusion.55
  477.5 2.6 fusion.19
  480.2 1.2 copy.109
  482.0 3.1 bitcast_convert_fusion
  485.2 1.2 copy.111
  486.4 1.8 copy.123
  488.2 1.3 constant_dynamic-update-slice_fusion.1
  489.5 56.1 %all-reduce.18.cloned.1.call-done = f32[512,768]{1,0:T(8,128)} async-done(((f32[512,768]{1,0:T(8,128)}), f32[512,768]{1,0:T(8,128)}) %all-reduce.18.cloned.1.call-update) | async-done | bytes 1572880 | tf_op jit(solution)/shard_map/psum | solution.py:193
  545.6 2.8 multiply_reduce_fusion.2
  549.0 1.1 copy-done.8
  553.6 1.7 convolution_convert_fusion.2
  555.4 1.3 constant_dynamic-update-slice_fusion
  556.6 7.2 convolution_convert_fusion
  565.0 3.8 fusion.93
  568.8 2.4 fusion.49
  571.2 5.5 convolution_bitcast_fusion.3
  576.8 1.1 pad_maximum_fusion.1
  578.3 1.1 fusion.53
  579.4 1.2 fusion.57
  581.5 1.3 pad_maximum_fusion
  583.5 1.3 fusion.61
  584.9 2.1 bitcast_reduce_fusion
  587.4 10.8 %all-reduce.20.cloned.1.call-done = bf16[512,768]{1,0:T(8,128)(2,1)} async-done(((bf16[512,768]{1,0:T(8,128)(2,1)}), bf16[512,768]{1,0:T(8,128)(2,1)}) %all-reduce.20.cloned.1.call-update) | async-done | bytes 786448 | tf_op jit(solution)/shard_map/psum | solution.py:223
  598.2 2.5 add_reduce_fusion
  600.8 25.6 %all-reduce = (f32[2,192]{1,0:T(2,128)}, f32[2,192]{1,0:T(2,128)}, f32[768]{0:T(1024)}, f32[1,768]{1,0:T(1,128)S(1)}, f32[1,768]{1,0:T(1,128)S(1)}, /*index=5*/f...) all-reduce(f32[2,192]{1,0:T(2,128)S(1)} %pad_maximum_fusion.11, ...), channel_id=1, replica_groups=mesh['dp'=8,'mp'=4] {'dp'}, use_global_device_ids=true, to_apply=%region_30.31 | all-reduce | flops 8448 | bytes 67584 | tf_op jit(solution)/shard_map/psum | solution.py:246
  628.2 82.3 %reduce-scatter.2.cloned.1.call-done = bf16[4096,192]{0,1:T(8,128)(2,1)} async-done(((bf16[4096,768]{0,1:T(8,128)(2,1)}), bf16[4096,192]{0,1:T(8,128)(2,1)}) %reduce-scatter.2.cloned.1.call-update) | async-done | bytes 1572880 | tf_op jit(solution)/shard_map/reduce_scatter | solution.py:197
  710.5 3.4 convert_element_type.157
  714.0 143.3 %all-reduce.22.cloned.1.call-done = (f32[3,768,192]{1,2,0:T(8,128)}, f32[192,768]{1,0:T(8,128)}, f32[768,192]{0,1:T(8,128)}, f32[2,768,192]{1,2,0:T(8,128)}, f32...) async-done(((f32[3,768,192]{1,2,0:T(8,128)}, f32[192,768]{1,0:T(8,128)}, f32[768,192]{0,1:T(8,128)}, f32[2,768,192]{1,2,0:T(8,128)}, f32[192,768]{1,0:T(8,128)}, ...) | async-done | bytes 9437200 | tf_op jit(solution)/shard_map/psum | solution.py:246
  857.3 2.9 copy.229
  861.8 1.0 copy.232
  864.2 1.4 copy.234
  865.6 1.1 copy-done.27
  866.7 1.4 copy.235
  (276 shorter events, 31.3 us)
Async XLA Ops:
  7.2 296.3 %copy-start = (bf16[768,768]{1,0:T(8,128)(2,1)S(1)}, bf16[768,768]{1,0:T(8,128)(2,1)}, u32[]{:S(2)}) copy-start(bf16[768,768]{1,0:T(8,128)(2,1)} %param.34) | copy-start | bytes 3538948
  7.2 2.2 copy-start.25
  7.2 79.8 %all-reduce.10.cloned.1.call-start = ((), (), s32[]{:S(2)}) async-start(), calls=%async_computation.1 | async-start | bytes 3145728 | tf_op jit(solution)/shard_map/psum | solution.py:140
  11.8 1.6 copy-start.41
  15.0 1.7 copy-start.51
  15.0 188.0 %all-gather.2.cloned.1.call-start = ((), (), s32[]{:S(2)}) async-start(), calls=%async_computation.2 | async-start | bytes 7864320 | tf_op jit(solution)/shard_map/all_gather | solution.py:150
  15.8 285.3 %all-reduce.12.cloned.1.call-start = ((), (), s32[]{:S(2)}) async-start(), calls=%async_computation.3 | async-start | bytes 3145728 | tf_op jit(solution)/shard_map/psum | solution.py:157
  16.1 364.2 %copy-start.63 = (f32[768]{0:T(1024)}, f32[768]{0:T(1024)S(1)}, u32[]{:S(2)}) copy-start(f32[768]{0:T(1024)S(1)} %get-tuple-element.122) | copy-start | bytes 9220
  16.7 211.4 %copy-start.12 = (pred[4,128,1024]{2,1,0:T(8,128)(4,1)}, pred[4,128,1024]{2,1,0:T(8,128)(4,1)S(1)}, u32[]{:S(2)}) copy-start(pred[4,128,1024]{2,1,0:T(8,128)(4,1)S(1)} %compare_and_fusion) | copy-start | bytes 1572868
  88.9 212.2 %copy-start.3 = (f32[512,768]{1,0:T(8,128)}, f32[512,768]{1,0:T(8,128)S(1)}, u32[]{:S(2)}) copy-start(f32[512,768]{1,0:T(8,128)S(1)} %get-tuple-element.170) | copy-start | bytes 4718596
  207.8 2.7 copy-start.17
  226.4 2.7 copy-start.2
  226.4 2.7 copy-start.21
  229.1 2.9 copy-start.39
  232.0 1.6 copy-start.37
  233.6 146.7 %all-reduce.14.cloned.1.call-start = ((), (), s32[]{:S(2)}) async-start(), calls=%async_computation.4 | async-start | bytes 3145728 | tf_op jit(solution)/shard_map/psum | solution.py:167
  303.1 6.1 copy-start.5
  303.8 6.3 copy-start.74
  312.0 68.3 %copy-start.6 = (f32[512,768]{1,0:T(8,128)S(1)}, f32[512,768]{1,0:T(8,128)}, u32[]{:S(2)}) copy-start(f32[512,768]{1,0:T(8,128)} %copy-done.5) | copy-start | bytes 4718596
  312.0 147.8 %all-reduce.16.cloned.1.call-start = ((), (), s32[]{:S(2)}) async-start(), calls=%async_computation.5 | async-start | bytes 3145728 | tf_op jit(solution)/shard_map/psum | solution.py:179
  384.2 1.6 copy-start.75
  384.2 1.9 copy-start.80
  384.2 2.5 copy-start.81
  385.8 2.7 copy-start.18
  391.5 154.1 %all-reduce.18.cloned.1.call-start = ((), (), s32[]{:S(2)}) async-start(), calls=%async_computation.6 | async-start | bytes 3145728 | tf_op jit(solution)/shard_map/psum | solution.py:193
  462.6 1.8 copy-start.40
  463.3 1.8 copy-start.13
  465.0 6.5 slice-start
  465.0 6.5 slice-start.1
  471.5 1.8 copy-start.19
  473.3 2.1 copy-start.14
  473.3 2.3 copy-start.62
  475.6 1.6 copy-start.33
  477.2 4.8 slice-start.2
  477.2 121.0 %all-reduce.20.cloned.1.call-start = ((), (), s32[]{:S(2)}) async-start(), calls=%async_computation.7 | async-start | bytes 1572864 | tf_op jit(solution)/shard_map/psum | solution.py:223
  477.5 4.5 slice-start.3
  488.2 57.4 %copy-start.4 = (f32[512,768]{1,0:T(8,128)S(1)}, f32[512,768]{1,0:T(8,128)}, u32[]{:S(2)}) copy-start(f32[512,768]{1,0:T(8,128)} %copy-done.3) | copy-start | bytes 4718596
  548.3 1.8 copy-start.42
  549.0 1.7 copy-start.16
  549.0 1.7 copy-start.50
  553.6 1.8 copy-start.20
  555.3 155.2 %reduce-scatter.2.cloned.1.call-start = ((), (), s32[]{:S(2)}) async-start(), calls=%async_computation.8 | async-start | bytes 7864320 | tf_op jit(solution)/shard_map/reduce_scatter | solution.py:197
  555.4 1.3 copy-start.43
  555.4 1.3 copy-start.44
  563.9 4.9 copy-start.7
  563.9 4.9 copy-start.64
  563.9 293.4 %all-reduce.22.cloned.1.call-start = ((), (), s32[]{:S(2)}) async-start(), calls=%async_computation.9 | async-start | bytes 18874368 | tf_op jit(solution)/shard_map/psum | solution.py:246
  565.0 3.8 copy-start.79
  568.8 2.4 copy-start.46
  576.7 1.4 copy-start.24
  576.7 1.6 copy-start.34
  576.8 2.7 copy-start.11
  576.8 2.7 copy-start.38
  581.4 2.1 copy-start.9
  581.5 2.1 copy-start.36
  584.8 2.2 copy-start.70
  587.4 13.4 %copy-start.68 = (f32[768]{0:T(1024)S(1)}, f32[768]{0:T(1024)}, u32[]{:S(2)}) copy-start(f32[768]{0:T(1024)} %get-tuple-element.210) | copy-start | bytes 9220
  857.3 2.9 copy-start.54
  857.3 3.7 copy-start.53
  860.2 1.6 copy-start.45
  861.0 1.8 copy-start.52
  861.8 2.3 copy-start.28
  864.2 2.5 copy-start.27
  864.2 3.9 copy-start.1
  (31 other events, 31.0 us)
Sparse Core Ops, SparseCore 0:
  15.2 71.7 all-reduce.9
  88.6 114.3 all-gather.1
  233.7 67.3 all-reduce.11
  312.2 68.1 all-reduce.13
  391.6 68.1 all-reduce.15
  477.4 68.1 all-reduce.17
  555.4 42.7 all-reduce.19
  600.5 109.9 reduce-scatter.1
  716.5 140.7 all-reduce.21
where the time goes:
time: 884 us; the launch traced here: 875 us
  waiting for transfers between devices  677 us (77%)
  matrix products  70.8 us (8%)
  local copies, waits for them, and re-layouts  47.4 us (5%)
  other arithmetic  37.7 us (4%)
  blocking collectives  25.6 us (3%)
  between operations  15.5 us (2%)
    psum x1, waiting for transfers between devices, body(): lax.psum((self_qkv_grad, self_qv_grad, self_proj_grad, cross_query_grad,...  143 us
    all_gather x1, waiting for transfers between devices, body(): memory_whole = lax.all_gather(memory, 'mp', axis=1, tiled=True)  110 us
    reduce_scatter x1, waiting for transfers between devices, body(): lax.psum_scatter(outer_dot(kv_grad_low, kv_weight).astype(jnp.bfloat16),...  82.3 us
    psum x1, waiting for transfers between devices, body(): lax.psum(jnp.dot(self_low, self_proj, preferred_element_type=jnp.float32)...  69.4 us
    psum x1, waiting for transfers between devices, body(): lax.psum(jnp.dot(activated_low, ffn_out, preferred_element_type=jnp.float...  68.3 us
    psum x1, waiting for transfers between devices, body(): second_grad = third_grad + lax.psum(outer_dot(pre_low, ffn_in), 'mp')  68.2 us
    psum x1, waiting for transfers between devices, body(): lax.psum(jnp.dot(cross_low, cross_proj, preferred_element_type=jnp.float3...  67.3 us
    psum x1, waiting for transfers between devices, body(): first_grad = cross_grad + lax.psum(outer_dot(cq_low, cross_query), 'mp')  56.1 us
  transfers between devices with their start and end apart: 9, of which 9 were waited for; matrix products, arithmetic and copies ran while one was open for 6% of the time, Pallas kernels for 0%

commit v1 on v0

--- a/solution.py
+++ b/solution.py
@@ -147,7 +147,18 @@
     first_low = first.astype(jnp.bfloat16)
     cross_pre = jnp.dot(first_low, cross_query, preferred_element_type=jnp.float32)
     cross_q = split_heads(((cross_pre + cross_qv_bias[0]) * scaling).astype(jnp.bfloat16))
-    memory_whole = lax.all_gather(memory, "mp", axis=1, tiled=True)
+    fan = lax.psum(1, "mp")
+    a_now = [(no - 1, no) for no in range(1, fan)] + [(fan - 1, 0)]
+    x_next = memory
+    pile = [x_next]
+    c = 0
+    while c < fan - 1:
+        x_next = lax.ppermute(x_next, axis_name="mp", perm=a_now)
+        pile += [x_next]
+        c += 1
+    fresh = jnp.concatenate([*reversed(pile)], axis=1)
+    v_next = lax.axis_index("mp")
+    memory_whole = jnp.roll(fresh, (v_next + 1) * x_next.shape[1], axis=1)
     kv_weight = jnp.concatenate([cross_kv[0], cross_kv[1]], axis=1)
     memory_kv = jnp.dot(memory_whole, kv_weight, preferred_element_type=jnp.float32)
     cross_k = split_heads(memory_kv[:, :local_width].astype(jnp.bfloat16))

time: 884 us -> 858 us (0.971)
  waiting for transfers between devices: 677 us -> 642 us
  local copies, waits for them, and re-layouts: 47.4 us -> 59.2 us
    all_gather x1 -> x0, waiting for transfers between devices: 110 us -> none  [body(): memory_whole = lax.all_gather(memory, 'mp', axis=1, tiled=True)]
    ppermute x0 -> x3, waiting for transfers between devices: none -> 89.7 us  [body(): x_next = lax.ppermute(x_next, axis_name='mp', perm=a_now)]
    psum x1, waiting for transfers between devices: 69.4 us -> 57.2 us  [body(): lax.psum(jnp.dot(self_low, self_proj, preferred_element_type=jnp.float32)...]
    unnamed x184 -> x211, local copies, waits for them, and re-layouts: 29.7 us -> 39.6 us
  transfers between devices with their start and end apart: 9 -> 11, of which waited for: 9 -> 10; matrix products, arithmetic and copies ran while one was open for 6% -> 7% of each run, Pallas kernels for 0% -> 0%
where the time goes in v1:
time: 858 us; the launch traced here: 854 us
  waiting for transfers between devices  642 us (75%)
  matrix products  68.8 us (8%)
  local copies, waits for them, and re-layouts  59.2 us (7%)
  other arithmetic  37.4 us (4%)
  blocking collectives  25.3 us (3%)
  between operations  16 us (2%)
    psum x1, waiting for transfers between devices, body(): lax.psum((self_qkv_grad, self_qv_grad, self_proj_grad, cross_query_grad,...  143 us
    ppermute x3, waiting for transfers between devices, body(): x_next = lax.ppermute(x_next, axis_name='mp', perm=a_now)  89.7 us
    reduce_scatter x1, waiting for transfers between devices, body(): lax.psum_scatter(outer_dot(kv_grad_low, kv_weight).astype(jnp.bfloat16),...  82.8 us
    psum x1, waiting for transfers between devices, body(): lax.psum(jnp.dot(activated_low, ffn_out, preferred_element_type=jnp.float...  68.3 us
    psum x1, waiting for transfers between devices, body(): second_grad = third_grad + lax.psum(outer_dot(pre_low, ffn_in), 'mp')  68 us
    psum x1, waiting for transfers between devices, body(): lax.psum(jnp.dot(cross_low, cross_proj, preferred_element_type=jnp.float3...  66.5 us
    psum x1, waiting for transfers between devices, body(): lax.psum(jnp.dot(self_low, self_proj, preferred_element_type=jnp.float32)...  57.2 us
    psum x1, waiting for transfers between devices, body(): first_grad = cross_grad + lax.psum(outer_dot(cq_low, cross_query), 'mp')  56 us
  transfers between devices with their start and end apart: 11, of which 10 were waited for; matrix products, arithmetic and copies ran while one was open for 7% of the time, Pallas kernels for 0%

profile of v1, /device:TPU:0, one launch (start us, length us, event | category | flops | bytes accessed | tf_op | source)
XLA Modules:
  0.0 853.5 jit_solution(17289624148021000973)
XLA Ops:
  7.3 3.1 collective-permute-start
  14.9 32.1 %collective-permute-done = bf16[4096,192]{0,1:T(8,128)(2,1)S(1)} collective-permute-done((bf16[4096,192]{0,1:T(8,128)(2,1)}, bf16[4096,192]{0,1:T(8,128)(2,1)S(1)}, u32[]{:S(2)}, u32[]{:S(2)}) %collective-permute-start) | collective-permute-done | bytes 1572896 | tf_op jit(solution)/shard_map/ppermute | solution.py:156
  47.1 1.6 fusion.67
  50.1 2.1 slice_bitcast_fusion.6
  52.2 57.7 %collective-permute-done.1 = bf16[4096,192]{0,1:T(8,128)(2,1)} collective-permute-done((bf16[4096,192]{0,1:T(8,128)(2,1)S(1)}, bf16[4096,192]{0,1:T(8,128)(2,1)}, u32[]{:S(2)}, u32[]{:S(2)}) %collective-permute-start.1) | collective-permute-done | bytes 1572896 | tf_op jit(solution)/shard_map/ppermute | solution.py:156
  110.4 57.2 %all-reduce.10.cloned.1.call-done = f32[512,768]{1,0:T(8,128)} async-done(((f32[512,768]{1,0:T(8,128)}), f32[512,768]{1,0:T(8,128)}) %all-reduce.10.cloned.1.call-update) | async-done | bytes 1572880 | tf_op jit(solution)/shard_map/psum | solution.py:140
  167.6 1.9 fusion.109
  173.1 1.5 constant_dynamic-update-slice_fusion.7
  174.7 1.6 constant_dynamic-update-slice_fusion.6
  176.7 1.3 copy-done.19
  178.1 1.5 constant_dynamic-update-slice_fusion.3
  179.6 1.5 constant_dynamic-update-slice_fusion.2
  182.3 2.6 fusion.3
  186.0 2.6 copy-done.24
  188.6 1.3 slice.156
  190.0 3.9 squeeze.90
  193.8 3.4 fusion.8
  197.2 3.9 squeeze.88
  201.0 3.5 select_reduce_fusion
  204.6 1.6 fusion
  207.2 2.8 fusion.43
  210.1 1.6 fusion.63
  212.0 66.5 %all-reduce.12.cloned.1.call-done = f32[512,768]{1,0:T(8,128)} async-done(((f32[512,768]{1,0:T(8,128)}), f32[512,768]{1,0:T(8,128)}) %all-reduce.12.cloned.1.call-update) | async-done | bytes 1572880 | tf_op jit(solution)/shard_map/psum | solution.py:168
  278.5 2.0 fusion.108
  281.2 5.4 multiply_convert_fusion.1
  287.5 1.9 fusion.121
  289.5 68.3 %all-reduce.14.cloned.1.call-done = f32[512,768]{1,0:T(8,128)} async-done(((f32[512,768]{1,0:T(8,128)}), f32[512,768]{1,0:T(8,128)}) %all-reduce.14.cloned.1.call-update) | async-done | bytes 1572880 | tf_op jit(solution)/shard_map/psum | solution.py:178
  357.8 2.0 fusion.106
  362.2 1.6 fusion.105
  364.7 1.8 fusion.116
  367.4 2.0 fusion.55
  369.7 68.0 %all-reduce.16.cloned.1.call-done = f32[512,768]{1,0:T(8,128)} async-done(((f32[512,768]{1,0:T(8,128)}), f32[512,768]{1,0:T(8,128)}) %all-reduce.16.cloned.1.call-update) | async-done | bytes 1572880 | tf_op jit(solution)/shard_map/psum | solution.py:190
  437.7 2.8 multiply_reduce_fusion.1
  443.0 6.5 multiply_reduce_fusion
  449.5 1.8 multiply_convert_fusion
  451.3 2.1 fusion.110
  453.6 1.6 fusion.59
  455.5 2.6 fusion.23
  458.2 1.2 copy.109
  460.0 3.2 bitcast_convert_fusion
  463.2 1.2 copy.111
  464.4 1.8 copy.123
  466.2 1.3 constant_dynamic-update-slice_fusion.9
  467.5 56.0 %all-reduce.18.cloned.1.call-done = f32[512,768]{1,0:T(8,128)} async-done(((f32[512,768]{1,0:T(8,128)}), f32[512,768]{1,0:T(8,128)}) %all-reduce.18.cloned.1.call-update) | async-done | bytes 1572880 | tf_op jit(solution)/shard_map/psum | solution.py:204
  523.5 2.8 multiply_reduce_fusion.2
  531.5 1.7 convolution_convert_fusion.2
  533.3 1.3 constant_dynamic-update-slice_fusion.8
  534.6 7.2 convolution_convert_fusion
  543.0 3.8 fusion.99
  546.7 2.4 fusion.53
  549.2 5.5 fusion.1
  557.5 1.3 fusion.61
  559.5 1.3 pad_maximum_fusion
  561.6 1.3 fusion.65
  563.5 2.1 bitcast_reduce_fusion
  566.1 10.1 %all-reduce.20.cloned.1.call-done = bf16[512,768]{1,0:T(8,128)(2,1)} async-done(((bf16[512,768]{1,0:T(8,128)(2,1)}), bf16[512,768]{1,0:T(8,128)(2,1)}) %all-reduce.20.cloned.1.call-update) | async-done | bytes 786448 | tf_op jit(solution)/shard_map/psum | solution.py:234
  576.1 2.5 add_reduce_fusion
  578.7 25.3 %all-reduce = (f32[2,192]{1,0:T(2,128)}, f32[2,192]{1,0:T(2,128)}, f32[768]{0:T(1024)}, f32[1,768]{1,0:T(1,128)S(1)}, f32[1,768]{1,0:T(1,128)S(1)}, /*index=5*/f...) all-reduce(f32[2,192]{1,0:T(2,128)S(1)} %pad_maximum_fusion.11, ...), channel_id=1, replica_groups=mesh['dp'=8,'mp'=4] {'dp'}, use_global_device_ids=true, to_apply=%region_30.31 | all-reduce | flops 8448 | bytes 67584 | tf_op jit(solution)/shard_map/psum | solution.py:257
  605.8 82.8 %reduce-scatter.2.cloned.1.call-done = bf16[4096,192]{0,1:T(8,128)(2,1)} async-done(((bf16[4096,768]{0,1:T(8,128)(2,1)}), bf16[4096,192]{0,1:T(8,128)(2,1)}) %reduce-scatter.2.cloned.1.call-update) | async-done | bytes 1572880 | tf_op jit(solution)/shard_map/reduce_scatter | solution.py:208
  688.6 3.4 convert_element_type.157
  692.0 143.3 %all-reduce.22.cloned.1.call-done = (f32[3,768,192]{1,2,0:T(8,128)}, f32[192,768]{1,0:T(8,128)}, f32[768,192]{0,1:T(8,128)}, f32[2,768,192]{1,2,0:T(8,128)}, f32...) async-done(((f32[3,768,192]{1,2,0:T(8,128)}, f32[192,768]{1,0:T(8,128)}, f32[768,192]{0,1:T(8,128)}, f32[2,768,192]{1,2,0:T(8,128)}, f32[192,768]{1,0:T(8,128)}, ...) | async-done | bytes 9437200 | tf_op jit(solution)/shard_map/psum | solution.py:257
  835.4 2.9 copy.236
  842.2 1.4 copy.241
  844.8 1.4 copy.242
  (307 shorter events, 42.3 us)
Async XLA Ops:
  7.2 273.7 %copy-start = (bf16[768,768]{1,0:T(8,128)(2,1)S(1)}, bf16[768,768]{1,0:T(8,128)(2,1)}, u32[]{:S(2)}) copy-start(bf16[768,768]{1,0:T(8,128)(2,1)} %param.34) | copy-start | bytes 3538948
  7.2 4.3 copy-start.80
  7.2 4.4 copy-start.28
  7.2 160.4 %all-reduce.10.cloned.1.call-start = ((), (), s32[]{:S(2)}) async-start(), calls=%async_computation.1 | async-start | bytes 3145728 | tf_op jit(solution)/shard_map/psum | solution.py:140
  7.3 39.7 %collective-permute-start = (bf16[4096,192]{0,1:T(8,128)(2,1)}, bf16[4096,192]{0,1:T(8,128)(2,1)S(1)}, u32[]{:S(2)}, u32[]{:S(2)}) collective-permute-start(bf16[4096,192]{0,1:T(8,128)(2,1)} %param.21), channel_id=1, source_target_pairs={{0,1},{1,2},{2,3},{3,0},{4,5},{5,6},{6,7},{7,4},{8,9},{9,10},{10,1... | collective-permute-start | bytes 4718600 | tf_op jit(solution)/shard_map/ppermute | solution.py:156
  14.0 33.0 %copy-start.44 = (bf16[192,768]{1,0:T(8,128)(2,1)S(1)}, bf16[192,768]{1,0:T(8,128)(2,1)}, u32[]{:S(2)}) copy-start(bf16[192,768]{1,0:T(8,128)(2,1)} %param.29) | copy-start | bytes 884740
  14.9 32.1 %copy-start.38 = (bf16[4,128,3,64]{1,0,3,2:T(4,128)(2,1)}, bf16[4,128,3,64]{1,0,3,2:T(4,128)(2,1)S(1)}, u32[]{:S(2)}) copy-start(bf16[4,128,3,64]{1,0,3,2:T(4,128)(2,1)S(1)} %copy.88) | copy-start | bytes 589828
  47.0 62.9 %collective-permute-start.1 = (bf16[4096,192]{0,1:T(8,128)(2,1)S(1)}, bf16[4096,192]{0,1:T(8,128)(2,1)}, u32[]{:S(2)}, u32[]{:S(2)}) collective-permute-start(bf16[4096,192]{0,1:T(8,128)(2,1)S(1)} %collective-permute-done), channel_id=1, source_target_pairs={{0,1},{1,2},{2,3},{3,0},{4,5},{5,6},{6,7},{7,4},{8,9},{9,10},{10,1... | collective-permute-start | bytes 4718600 | tf_op jit(solution)/shard_map/ppermute | solution.py:156
  47.0 1.9 copy-start.74
  47.0 1.9 copy-start.75
  47.0 2.5 copy-start.82
  47.0 2.5 copy-start.83
  47.1 2.6 copy-start.69
  48.6 61.7 %copy-start.76 = (f32[3,768]{1,0:T(4,128)S(1)}, f32[3,768]{1,0:T(4,128)}, u32[]{:S(2)}) copy-start(f32[3,768]{1,0:T(4,128)} %param.37) | copy-start | bytes 27652
  48.7 229.8 %all-reduce.12.cloned.1.call-start = ((), (), s32[]{:S(2)}) async-start(), calls=%async_computation.2 | async-start | bytes 3145728 | tf_op jit(solution)/shard_map/psum | solution.py:168
  50.1 156.1 %copy-start.12 = (pred[4,128,1024]{2,1,0:T(8,128)(4,1)}, pred[4,128,1024]{2,1,0:T(8,128)(4,1)S(1)}, u32[]{:S(2)}) copy-start(pred[4,128,1024]{2,1,0:T(8,128)(4,1)S(1)} %compare_and_fusion) | copy-start | bytes 1572868
  109.8 63.3 %collective-permute-start.2 = (bf16[4096,192]{0,1:T(8,128)(2,1)}, bf16[4096,192]{0,1:T(8,128)(2,1)}, u32[]{:S(2)}, u32[]{:S(2)}) collective-permute-start(bf16[4096,192]{0,1:T(8,128)(2,1)} %collective-permute-done.1), channel_id=1, source_target_pairs={{0,1},{1,2},{2,3},{3,0},{4,5},{5,6},{6,7},{7,4},{8,9},{9,10},{10,1... | collective-permute-start | bytes 4718600 | tf_op jit(solution)/shard_map/ppermute | solution.py:156
  169.5 109.0 %copy-start.3 = (f32[512,768]{1,0:T(8,128)}, f32[512,768]{1,0:T(8,128)S(1)}, u32[]{:S(2)}) copy-start(f32[512,768]{1,0:T(8,128)S(1)} %get-tuple-element.170) | copy-start | bytes 4718596
  174.7 1.9 copy-start.21
  181.5 4.6 copy-start.67
  186.0 2.6 copy-start.24
  204.5 2.7 copy-start.2
  204.5 2.7 copy-start.23
  207.2 2.9 copy-start.42
  211.7 146.1 %all-reduce.14.cloned.1.call-start = ((), (), s32[]{:S(2)}) async-start(), calls=%async_computation.3 | async-start | bytes 3145728 | tf_op jit(solution)/shard_map/psum | solution.py:178
  280.5 6.2 copy-start.5
  281.2 6.3 copy-start.84
  289.5 68.4 %copy-start.6 = (f32[512,768]{1,0:T(8,128)S(1)}, f32[512,768]{1,0:T(8,128)}, u32[]{:S(2)}) copy-start(f32[512,768]{1,0:T(8,128)} %copy-done.5) | copy-start | bytes 4718596
  289.5 148.2 %all-reduce.16.cloned.1.call-start = ((), (), s32[]{:S(2)}) async-start(), calls=%async_computation.4 | async-start | bytes 3145728 | tf_op jit(solution)/shard_map/psum | solution.py:190
  360.1 2.0 copy-start.71
  362.2 1.9 copy-start.90
  362.2 2.5 copy-start.91
  363.8 2.7 copy-start.17
  369.4 154.1 %all-reduce.18.cloned.1.call-start = ((), (), s32[]{:S(2)}) async-start(), calls=%async_computation.5 | async-start | bytes 3145728 | tf_op jit(solution)/shard_map/psum | solution.py:204
  440.5 1.9 copy-start.43
  441.2 1.8 copy-start.13
  442.9 6.5 slice-start
  443.0 6.5 slice-start.1
  449.5 1.8 copy-start.18
  451.3 2.1 copy-start.14
  451.3 2.3 copy-start.62
  455.2 4.9 slice-start.2
  455.2 120.9 %all-reduce.20.cloned.1.call-start = ((), (), s32[]{:S(2)}) async-start(), calls=%async_computation.6 | async-start | bytes 1572864 | tf_op jit(solution)/shard_map/psum | solution.py:234
  455.5 4.5 slice-start.3
  466.2 57.3 %copy-start.4 = (f32[512,768]{1,0:T(8,128)S(1)}, f32[512,768]{1,0:T(8,128)}, u32[]{:S(2)}) copy-start(f32[512,768]{1,0:T(8,128)} %copy-done.3) | copy-start | bytes 4718596
  531.5 1.8 copy-start.22
  533.3 155.3 %reduce-scatter.2.cloned.1.call-start = ((), (), s32[]{:S(2)}) async-start(), calls=%async_computation.7 | async-start | bytes 7864320 | tf_op jit(solution)/shard_map/reduce_scatter | solution.py:208
  541.8 4.9 copy-start.7
  541.9 4.9 copy-start.73
  541.9 293.5 %all-reduce.22.cloned.1.call-start = ((), (), s32[]{:S(2)}) async-start(), calls=%async_computation.8 | async-start | bytes 18874368 | tf_op jit(solution)/shard_map/psum | solution.py:257
  543.0 3.8 copy-start.89
  546.7 2.4 copy-start.47
  554.8 2.7 copy-start.11
  554.8 2.7 copy-start.41
  559.5 2.1 copy-start.9
  559.5 2.1 copy-start.39
  563.5 2.2 copy-start.79
  566.0 12.6 %copy-start.77 = (f32[768]{0:T(1024)S(1)}, f32[768]{0:T(1024)}, u32[]{:S(2)}) copy-start(f32[768]{0:T(1024)} %get-tuple-element.210) | copy-start | bytes 9220
  835.4 2.9 copy-start.54
  835.4 3.7 copy-start.53
  839.1 1.8 copy-start.52
  839.9 2.3 copy-start.31
  842.2 2.5 copy-start.30
  842.2 3.9 copy-start.1
  (43 other events, 51.4 us)
Sparse Core Ops, SparseCore 0:
  48.8 118.7 all-reduce.9
  211.8 66.6 all-reduce.11
  289.6 68.1 all-reduce.13
  369.5 68.1 all-reduce.15
  455.3 68.1 all-reduce.17
  533.4 42.7 all-reduce.19
  578.4 110.1 reduce-scatter.1
  694.5 140.7 all-reduce.21
